TPU v7x, 32 devices: a whole 2x2x4 slice. The times are simulated.
32 devices in a mesh: copy: 2 (over y), grid: 4 (over z), blk: 2 (over x), sub: 2 (over core).
Axes of the slice: x: 2, y: 2, z: 4, core: 2. Of those that a mesh axis runs over, the one named last changes fastest.
Arguments:
- ensemble: float32 [128, 3, 256, 1024], P(('copy', 'grid'), None, 'blk', 'sub'), parts along dimension 0, may hold values from -6 to 6
- basin_thickness: float32 [512, 1024], P(('copy', 'blk'), 'sub'), parts along dimension 0, may hold values from 0.25 to 2
- wet_indicator: int32 [512, 1024], P(('copy', 'blk'), 'sub'), parts along dimension 0, may hold values 0 or 1
- obs_cell: int32 [4, 4, 2, 64], P(('copy', 'blk'), 'grid', 'sub'), parts along dimension 0, may hold values from 0 to 16383
- obs_count: int32 [4, 4, 2], P(('copy', 'blk'), 'grid', 'sub'), parts along dimension 0, may hold values from 16 to 64, as said below
- obs_value: float32 [4, 4, 2, 64], P(('copy', 'blk'), 'grid', 'sub'), parts along dimension 0, may hold values from -6 to 6
- obs_error: float32 [4, 4, 2, 64], P(('copy', 'blk'), 'grid', 'sub'), parts along dimension 0, may hold values from 0.5 to 2
Outputs:
- analysis: float32 [128, 3, 2, 128, 1024], P('copy', None, 'blk', 'grid', 'sub'), parts along dimension 0
There are 2 independent parts, one for each index of `copy`. A program takes and returns all parts, laid end to end along the dimension named above; each array names one. Nothing has to cross between parts.
Inputs may be any that keep to these rules, and one draw needn't show every extreme that they name: `obs_count`: one block of every draw has all 64 slots live.
All inputs are finite; a program needn't handle non-finite values. No bound on the sum of `wet_indicator` on one device may be relied on, other than what follows from the above.
Results may differ from a plain program's by a relative error of at most 0.0003.
Values sent between devices are 32-bit elements; how exact they have to be, the bound alone decides.
No kernel may reach another device: no remote copies, remote signals or barrier semaphores. Data moves between devices by JAX's collectives and lax.ppermute only.
A program may use at most 128 MiB of HBM per device.

v0:
```python
import math
import jax
import jax.numpy as jnp
from jax import lax
from jax.sharding import PartitionSpec as P

STEPS = 2
NS_STEPS = 8
FRICTION = 0.05
PRESSURE = 0.35
DIVERGE = 0.35
CORIOLIS = 0.2
precise = lax.Precision.HIGHEST


def padded(cells, sides, width):
    for axis, dim in sides:
        count = lax.axis_size(axis)
        ends = count - 1
        head = lax.slice_in_dim(cells, 0, width, axis=dim)
        tail = lax.slice_in_dim(cells, cells.shape[dim] - width, cells.shape[dim], axis=dim)
        cells = jnp.concatenate(
            [
                lax.ppermute(tail, axis, [(i, (i + 1) % count) for i in range(ends)]),
                cells,
                lax.ppermute(head, axis, [((i + 1) % count, i) for i in range(ends)]),
            ],
            axis=dim,
        )
    return cells


def thin_step(dynamic_vector, static_local, inner_cor):
    height = dynamic_vector[:, 0]
    bordered_array = padded(height, (("blk", 1), ("sub", 2)), 1)
    inner_depth = static_local[0]
    interior_indicator = static_local[1]
    grad_first = bordered_array[:, 2:, 1:-1] - bordered_array[:, :-2, 1:-1]
    grad_second = bordered_array[:, 1:-1, 2:] - bordered_array[:, 1:-1, :-2]
    first_new = interior_indicator * (
        (1.0 - FRICTION) * dynamic_vector[:, 1]
        + inner_cor * dynamic_vector[:, 2]
        - PRESSURE * grad_first
    )
    second_new = interior_indicator * (
        (1.0 - FRICTION) * dynamic_vector[:, 2]
        - inner_cor * dynamic_vector[:, 1]
        - PRESSURE * grad_second
    )
    fluxes = jnp.stack([inner_depth * first_new, inner_depth * second_new], axis=1)
    flux_wide = padded(fluxes, (("blk", 2), ("sub", 3)), 1)
    divergence = (
        flux_wide[:, 0, 2:, 1:-1]
        - flux_wide[:, 0, :-2, 1:-1]
        + (flux_wide[:, 1, 1:-1, 2:] - flux_wide[:, 1, 1:-1, :-2])
    )
    height_new = height - DIVERGE * divergence
    return jnp.stack([height_new, first_new, second_new], axis=1)


def observe(surface_height, obs_cell, obs_count, obs_value, obs_error):
    members = surface_height.shape[0]
    flat = surface_height.reshape(members, -1)
    cells = obs_cell.reshape(-1)
    picked = jnp.take(flat, cells, axis=1)
    pbar = jnp.mean(picked, axis=0)
    valid = jnp.arange(cells.shape[0], dtype=jnp.int32) < obs_count.reshape(())
    scale = jnp.where(valid, 1.0 / (obs_error.reshape(-1) * math.sqrt(members - 1)), 0.0)
    anomobs = (picked - pbar) * scale
    innov = (obs_value.reshape(-1) - pbar) * scale
    gram = jnp.dot(anomobs, anomobs.T, precision=precise)
    proj = jnp.dot(anomobs, innov, precision=precise)
    return jnp.concatenate([gram, proj[None]], axis=0)


def domain_reduction(packed):
    packed = lax.psum(packed, ("blk", "sub"))
    return packed


def transform(packed):
    members = packed.shape[1]
    eye = jnp.eye(members, dtype=jnp.float32)
    system = eye + packed[:members]
    proj = packed[members]
    factor_low = jnp.linalg.cholesky(system)
    mean_w = jax.scipy.linalg.cho_solve((factor_low, True), proj)
    scale = jnp.sqrt(jnp.sum(system * system))
    ystate = system / scale
    zstate = eye
    for sweep in range(NS_STEPS):
        factor = 1.5 * eye - 0.5 * jnp.dot(zstate, ystate, precision=precise)
        ystate = jnp.dot(ystate, factor, precision=precise)
        zstate = jnp.dot(factor, zstate, precision=precise)
    return mean_w[:, None] + zstate / jnp.sqrt(scale)


def shards(ensemble, basin_thickness, wet_indicator, obs_cell, obs_count, obs_value, obs_error):
    rows_dev = ensemble.shape[2]
    constant_fields = jnp.stack([basin_thickness, wet_indicator.astype(jnp.float32)])
    total_rows = rows_dev * lax.axis_size("blk")
    rows = (
        lax.axis_index("blk") * rows_dev + jnp.arange(-2, rows_dev + 2, dtype=jnp.int32)
    ).astype(jnp.float32)
    latitude_coupling = (CORIOLIS * (2.0 * (rows + 0.5) / total_rows - 1.0))[:, None]
    dynamic_vector = ensemble
    inner_cor = latitude_coupling[2:-2]
    for number in range(STEPS):
        dynamic_vector = thin_step(dynamic_vector, constant_fields, inner_cor)
    blocks = lax.all_to_all(dynamic_vector, "grid", split_axis=2, concat_axis=0, tiled=True)
    packed = domain_reduction(observe(blocks[:, 0], obs_cell, obs_count, obs_value, obs_error))
    weights = transform(packed)
    members = blocks.shape[0]
    flat = blocks.reshape(members, -1)
    center = jnp.mean(flat, axis=0)
    member_deviations = flat - center
    updated = center + jnp.dot(weights.T, member_deviations, precision=precise)
    return updated.reshape(members, 3, 1, blocks.shape[2], blocks.shape[3])


def solution(mesh):
    placed = (
        P(("copy", "grid"), None, "blk", "sub"),
        P(("copy", "blk"), "sub"),
        P(("copy", "blk"), "sub"),
        P(("copy", "blk"), "grid", "sub", None),
        P(("copy", "blk"), "grid", "sub"),
        P(("copy", "blk"), "grid", "sub", None),
        P(("copy", "blk"), "grid", "sub", None),
    )
    return jax.shard_map(
        shards,
        mesh=mesh,
        in_specs=placed,
        out_specs=P("copy", None, "blk", "grid", "sub"),
        check_vma=False,
    )
```

profile of v0, /device:TPU:0, one launch (start us, length us, event | category | flops | bytes accessed | tf_op | source)
XLA Modules:
  0.0 581.9 jit_solution(4712304430399835638)
XLA Ops:
  0.0 10.2 %fusion.67 = (f32[16,1,128,512]{3,2,1,0:T(8,128)}, f32[16,1,128,512]{3,2,1,0:T(8,128)}, f32[16,1,128,512]{3,2,1,0:T(8,128)S(1)}) fusion(f32[16,3,128,512]{3,2,1,0:T(8,128)} %param.7), kind=kLoop, calls=%fused_computation.164 | loop fusion | bytes 25165824 | tf_op jit(solution)/shard_map/slice | solution.py:42
  15.9 4.8 collective-permute-start.1
  32.1 21.8 %multiply_bitcast_fusion.3 = (f32[16,1,128,512]{3,0,2,1:T(8,128)S(1)}, f32[16,128,512]{2,0,1:T(8,128)}, f32[16,1,128,512]{3,0,2,1:T(8,128)}, f32[16,128,512]{2,0,1:T(8,128)}) fusion(f32[128,512]{1,0:T(8,128)S(1)} %copy-done.8, f32[16,128,512]{2,0,1:T(8,128)} %bitcast.143, f32[16,1,512]{2,0,1:T(8,128)S(1)} %collective-permute-done.1, ...), kind=kLoop, calls=%fused_computation.76 | loop fusion | flops 25165824 | bytes 29967104 | tf_op jit(solution)/shard_map/stack | solution.py:50
  56.5 4.7 collective-permute-start.5
  79.9 11.1 %bitcast_subtract_fusion = (f32[16,128,512]{2,0,1:T(8,128)S(1)}, f32[16,1,128,512]{3,0,2,1:T(8,128)}) fusion(f32[16,1,128,512]{3,2,1,0:T(8,128)} %copy-done.4, f32[16,2,1,512]{3,0,2,1:T(8,128)S(1)} %collective-permute-done.4, f32[16,1,128,512]{3,0,2,1:T(8,128)} %get-tuple-element.17, f32[16,1,128,512]{3,0,2,1:T(8,128)} %copy-done.2, ...), kind=kLoop, calls=%fused_computation.72 | loop fusion | flops 17825792 | bytes 21135872 | tf_op jit(solution)/shard_map/sub | solution.py:57
  92.3 4.5 collective-permute-start.9
  106.1 17.2 %multiply_bitcast_fusion.1 = (f32[16,1,128,512]{3,0,2,1:T(8,128)S(1)}, f32[16,128,512]{2,0,1:T(8,128)}, f32[16,1,128,512]{3,0,2,1:T(8,128)S(1)}, f32[16,128,512]{2,0,1:T(8,128)}) fusion(f32[128,512]{1,0:T(8,128)} %param.8, f32[16,128,512]{2,0,1:T(8,128)} %copy-done.6, f32[16,1,512]{2,0,1:T(8,128)S(1)} %collective-permute-done.9, ...), kind=kLoop, calls=%fused_computation.74 | loop fusion | flops 25165824 | bytes 29967104 | tf_op jit(solution)/shard_map/stack | solution.py:50
  124.7 4.5 collective-permute-start.13
  146.1 13.0 %fusion.5 = f32[16,1,128,512]{3,0,2,1:T(8,128)} fusion(f32[16,2,130,1]{3,0,2,1:T(8,128)} %copy.66, f32[16,2,1,512]{3,0,2,1:T(8,128)S(1)} %collective-permute-done.12, f32[16,2,1,512]{3,0,2,1:T(8,128)S(1)} %collective-permute-done.13, f32[16,1,128,512]{3,0,2,1:T(8,128)} %copy-done.1, f32[16,1,128,512]{3,0,2,1:T(8,128)} %copy-done, ...), kind=kLoop, calls=%fused_computation.9 | loop fusion | flops 18874368 | bytes 21135872 | tf_op jit(solution)/shard_map/sub | solution.py:57
  159.1 9.0 %pad_maximum_fusion = f32[16,3,128,512]{3,0,2,1:T(8,128)} fusion(f32[16,1,128,512]{3,0,2,1:T(8,128)} %bitcast.145, f32[16,1,128,512]{3,0,2,1:T(8,128)S(1)} %bitcast.144, f32[16,1,128,512]{3,0,2,1:T(8,128)} %fusion.5), kind=kLoop, calls=%fused_computation.2 | loop fusion | flops 6291456 | bytes 25165824 | tf_op jit(solution)/shard_map/stack | solution.py:58
  168.2 12.1 %copy.67 = f32[16,3,128,512]{3,0,1,2:T(8,128)} copy(f32[16,3,128,512]{3,0,2,1:T(8,128)} %pad_maximum_fusion) | data formatting | bytes 25165824 | tf_op jit(solution)/shard_map/stack | solution.py:58
  180.2 6.8 %all-to-all-start = ((f32[16,3,128,512]{3,0,1,2:T(8,128)}), f32[16,3,128,512]{3,0,1,2:T(8,128)}, u32[]{:S(2)}, u32[]{:S(2)}) async-start(f32[16,3,128,512]{3,0,1,2:T(8,128)} %copy.67), calls=%async_computation | async-start | bytes 25165824 | tf_op jit(solution)/shard_map/all_to_all | solution.py:110
  187.9 273.5 %all-to-all-done = f32[16,3,128,512]{3,0,1,2:T(8,128)} async-done(((f32[16,3,128,512]{3,0,1,2:T(8,128)}), f32[16,3,128,512]{3,0,1,2:T(8,128)}, u32[]{:S(2)}, u32[]{:S(2)}) %all-to-all-start) | async-done | bytes 12582944 | tf_op jit(solution)/shard_map/all_to_all | solution.py:110
  461.4 16.6 %copy.108 = f32[16,3,4,32,512]{4,3,1,0,2:T(8,128)} copy(f32[16,3,4,32,512]{4,0,1,3,2:T(8,128)} %bitcast.10) | data formatting | bytes 25165824 | tf_op jit(solution)/shard_map/all_to_all | solution.py:110
  478.0 5.0 slice.199
  483.0 6.9 %copy.79 = f32[64,1,32,512]{0,3,2,1:T(8,128)} copy(f32[64,1,32,512]{3,2,1,0:T(8,128)} %slice.199) | data formatting | bytes 8388608
  490.0 4.0 gather_fusion
  494.9 11.5 %psum.7 = f32[65,64]{0,1:T(8,128)S(1)} all-reduce(f32[65,64]{0,1:T(8,128)S(1)} %pad_maximum_fusion.59), channel_id=1, replica_groups=mesh['copy'=2,'grid'=4,'blk'=2,'sub'=2] {'blk','sub'}, use_global_device_ids=true, to_apply=%region_2.3 | all-reduce | flops 4160 | bytes 33280 | tf_op jit(solution)/shard_map/psum | solution.py:77
  511.6 11.1 %bitcast_reduce_fusion = f32[3,32,512]{2,1,0:T(8,128)S(1)} fusion(f32[16,3,4,32,512]{4,0,1,3,2:T(8,128)} %bitcast.10), kind=kLoop, calls=%fused_computation.160 | loop fusion | flops 3096576 | bytes 12779520 | tf_op jit(solution)/shard_map/reduce_sum | solution.py:115
  522.8 5.8 %cholesky.26 = f32[64,64]{1,0:T(8,128)S(1)} custom-call(f32[64,64]{1,0:T(8,128)S(1)} %fusion.39), custom_call_target="Cholesky" | custom-call | tf_op jit(solution)/shard_map/jit(cholesky)/cholesky | solution.py:86
  530.1 4.9 custom-call.10
  535.4 12.0 %reshape.118 = f32[64,49152]{1,0:T(8,128)} reshape(f32[4,16,3,32,512]{4,3,2,1,0:T(8,128)} %bitcast.139) | data formatting | bytes 25165824 | tf_op jit(solution)/shard_map/reshape | solution.py:114
  547.8 17.4 %convolution_add_fusion = f32[64,49152]{1,0:T(8,128)} fusion(f32[64,64]{1,0:T(8,128)S(1)} %fusion.28, f32[64,49152]{1,0:T(8,128)} %reshape.118, f32[49152]{0:T(1024)S(1)} %bitcast.147), kind=kOutput, calls=%fused_computation.1 | convolution fusion | flops 2422210560 | bytes 25378816 | tf_op jit(solution)/shard_map/dot_general | solution.py:117
  565.2 16.4 %copy.85 = f32[8,8,96,512]{3,2,1,0:T(8,128)} copy(f32[8,8,96,512]{3,1,2,0:T(8,128)} %bitcast.140) | data formatting | bytes 25165824
  (127 shorter events, 74.5 us)
Async XLA Ops:
  14.7 6.2 %collective-permute-start = (f32[16,1,512]{2,0,1:T(8,128)S(1)}, f32[16,1,512]{2,0,1:T(8,128)S(1)}, u32[]{:S(2)}, u32[]{:S(2)}) collective-permute-start(f32[16,1,512]{2,0,1:T(8,128)S(1)} %get-tuple-element.39), channel_id=1, source_target_pairs={{2,0},{3,1},{6,4},{7,5},{10,8},{11,9},{14,12},{15,13},{18,16},{19,... | collective-permute-start | bytes 98312 | tf_op jit(solution)/shard_map/ppermute | solution.py:26
  15.9 6.4 %collective-permute-start.1 = (f32[16,1,512]{2,0,1:T(8,128)S(1)}, f32[16,1,512]{2,0,1:T(8,128)S(1)}, u32[]{:S(2)}, u32[]{:S(2)}) collective-permute-start(f32[16,1,512]{2,0,1:T(8,128)S(1)} %get-tuple-element.38), channel_id=1, source_target_pairs={{0,2},{1,3},{4,6},{5,7},{8,10},{9,11},{12,14},{13,15},{16,18},{17,... | collective-permute-start | bytes 98312 | tf_op jit(solution)/shard_map/ppermute | solution.py:24
  20.8 9.6 %copy-start.9 = (s32[128,512]{1,0:T(8,128)S(1)}, s32[128,512]{1,0:T(8,128)}, u32[]{:S(2)}) copy-start(s32[128,512]{1,0:T(8,128)} %param.9) | copy-start | bytes 786436
  20.8 11.3 %copy-start.8 = (f32[128,512]{1,0:T(8,128)S(1)}, f32[128,512]{1,0:T(8,128)}, u32[]{:S(2)}) copy-start(f32[128,512]{1,0:T(8,128)} %param.8) | copy-start | bytes 786436
  24.9 5.6 collective-permute-start.2
  26.9 4.4 collective-permute-start.3
  53.9 9.2 %copy-start.2 = (f32[16,1,128,512]{3,0,2,1:T(8,128)}, f32[16,1,128,512]{3,0,2,1:T(8,128)S(1)}, u32[]{:S(2)}) copy-start(f32[16,1,128,512]{3,0,2,1:T(8,128)S(1)} %get-tuple-element.11) | copy-start | bytes 12582916
  53.9 9.2 %copy-start.3 = (f32[16,1,128,512]{3,0,2,1:T(8,128)S(1)}, f32[16,1,128,512]{3,0,2,1:T(8,128)}, u32[]{:S(2)}) copy-start(f32[16,1,128,512]{3,0,2,1:T(8,128)} %get-tuple-element.17) | copy-start | bytes 12582916
  55.0 6.6 %collective-permute-start.4 = (f32[16,2,1,512]{3,0,2,1:T(8,128)S(1)}, f32[16,2,1,512]{3,0,2,1:T(8,128)S(1)}, u32[]{:S(2)}, u32[]{:S(2)}) collective-permute-start(f32[16,2,1,512]{3,0,2,1:T(8,128)S(1)} %get-tuple-element.31), channel_id=1, source_target_pairs={{2,0},{3,1},{6,4},{7,5},{10,8},{11,9},{14,12},{15,13},{18,16},{19,... | collective-permute-start | bytes 196616 | tf_op jit(solution)/shard_map/ppermute | solution.py:26
  56.5 6.6 %collective-permute-start.5 = (f32[16,2,1,512]{3,0,2,1:T(8,128)S(1)}, f32[16,2,1,512]{3,0,2,1:T(8,128)S(1)}, u32[]{:S(2)}, u32[]{:S(2)}) collective-permute-start(f32[16,2,1,512]{3,0,2,1:T(8,128)S(1)} %get-tuple-element.30), channel_id=1, source_target_pairs={{0,2},{1,3},{4,6},{5,7},{8,10},{9,11},{12,14},{13,15},{16,18},{17,... | collective-permute-start | bytes 196616 | tf_op jit(solution)/shard_map/ppermute | solution.py:24
  68.1 7.0 %collective-permute-start.6 = (f32[16,2,130,1]{2,0,3,1:T(8,128)S(1)}, f32[16,2,130,1]{2,0,3,1:T(8,128)}, u32[]{:S(2)}, u32[]{:S(2)}) collective-permute-start(f32[16,2,130,1]{2,0,3,1:T(8,128)S(1)} %copy.55), channel_id=1, source_target_pairs={{1,0},{3,2},{5,4},{7,6},{9,8},{11,10},{13,12},{15,14},{17,16},{19,... | collective-permute-start | bytes 49928 | tf_op jit(solution)/shard_map/ppermute | solution.py:26
  71.2 6.0 %collective-permute-start.7 = (f32[16,2,130,1]{2,0,3,1:T(8,128)}, f32[16,2,130,1]{2,0,3,1:T(8,128)S(1)}, u32[]{:S(2)}, u32[]{:S(2)}) collective-permute-start(f32[16,2,130,1]{2,0,3,1:T(8,128)} %copy.57), channel_id=1, source_target_pairs={{0,1},{2,3},{4,5},{6,7},{8,9},{10,11},{12,13},{14,15},{16,17},{18,... | collective-permute-start | bytes 49928 | tf_op jit(solution)/shard_map/ppermute | solution.py:24
  91.0 5.9 %collective-permute-start.8 = (f32[16,1,512]{2,0,1:T(8,128)S(1)}, f32[16,1,512]{2,0,1:T(8,128)S(1)}, u32[]{:S(2)}, u32[]{:S(2)}) collective-permute-start(f32[16,1,512]{2,0,1:T(8,128)S(1)} %get-tuple-element.37), channel_id=1, source_target_pairs={{2,0},{3,1},{6,4},{7,5},{10,8},{11,9},{14,12},{15,13},{18,16},{19,... | collective-permute-start | bytes 98312 | tf_op jit(solution)/shard_map/ppermute | solution.py:26
  92.3 6.1 %collective-permute-start.9 = (f32[16,1,512]{2,0,1:T(8,128)S(1)}, f32[16,1,512]{2,0,1:T(8,128)S(1)}, u32[]{:S(2)}, u32[]{:S(2)}) collective-permute-start(f32[16,1,512]{2,0,1:T(8,128)S(1)} %get-tuple-element.36), channel_id=1, source_target_pairs={{0,2},{1,3},{4,6},{5,7},{8,10},{9,11},{12,14},{13,15},{16,18},{17,... | collective-permute-start | bytes 98312 | tf_op jit(solution)/shard_map/ppermute | solution.py:24
  99.5 5.0 collective-permute-start.10
  101.5 3.9 collective-permute-start.11
  123.4 6.2 %collective-permute-start.12 = (f32[16,2,1,512]{3,0,2,1:T(8,128)S(1)}, f32[16,2,1,512]{3,0,2,1:T(8,128)S(1)}, u32[]{:S(2)}, u32[]{:S(2)}) collective-permute-start(f32[16,2,1,512]{3,0,2,1:T(8,128)S(1)} %get-tuple-element.29), channel_id=1, source_target_pairs={{2,0},{3,1},{6,4},{7,5},{10,8},{11,9},{14,12},{15,13},{18,16},{19,... | collective-permute-start | bytes 196616 | tf_op jit(solution)/shard_map/ppermute | solution.py:26
  124.7 6.4 %collective-permute-start.13 = (f32[16,2,1,512]{3,0,2,1:T(8,128)S(1)}, f32[16,2,1,512]{3,0,2,1:T(8,128)S(1)}, u32[]{:S(2)}, u32[]{:S(2)}) collective-permute-start(f32[16,2,1,512]{3,0,2,1:T(8,128)S(1)} %get-tuple-element.28), channel_id=1, source_target_pairs={{0,2},{1,3},{4,6},{5,7},{8,10},{9,11},{12,14},{13,15},{16,18},{17,... | collective-permute-start | bytes 196616 | tf_op jit(solution)/shard_map/ppermute | solution.py:24
  136.2 5.8 collective-permute-start.14
  138.9 4.5 collective-permute-start.15
  146.1 13.0 %copy-start.7 = (f32[16,128,512]{2,0,1:T(8,128)S(1)}, f32[16,128,512]{2,0,1:T(8,128)}, u32[]{:S(2)}) copy-start(f32[16,128,512]{2,0,1:T(8,128)} %get-tuple-element.6) | copy-start | bytes 12582916
  180.2 281.1 %all-to-all-start = ((f32[16,3,128,512]{3,0,1,2:T(8,128)}), f32[16,3,128,512]{3,0,1,2:T(8,128)}, u32[]{:S(2)}, u32[]{:S(2)}) async-start(f32[16,3,128,512]{3,0,1,2:T(8,128)} %copy.67), calls=%async_computation | async-start | bytes 25165824 | tf_op jit(solution)/shard_map/all_to_all | solution.py:110
  483.0 11.1 %copy-start.10 = (f32[1,1,1,64]{3,2,1,0:T(1,128)S(1)}, f32[1,1,1,64]{3,2,1,0:T(1,128)}, u32[]{:S(2)}) copy-start(f32[1,1,1,64]{3,2,1,0:T(1,128)} %param.13) | copy-start | bytes 772
  483.0 11.4 %copy-start.12 = (f32[1,1,1,64]{3,2,1,0:T(1,128)S(1)}, f32[1,1,1,64]{3,2,1,0:T(1,128)}, u32[]{:S(2)}) copy-start(f32[1,1,1,64]{3,2,1,0:T(1,128)} %param.12) | copy-start | bytes 772
  (6 other events, 35.0 us)
where the time goes:
time: 588 us; the launch traced here: 582 us
  waiting for transfers between devices  280 us (48%)
  local copies, waits for them, and re-layouts  112 us (19%)
  other arithmetic  104 us (18%)
  starting transfers between devices  49.6 us (8%)
  matrix products  22.2 us (4%)
  blocking collectives  11.5 us (2%)
    all_to_all x1, waiting for transfers between devices, shards(): lax.all_to_all(dynamic_vector, 'grid', split_axis=2, concat_axis=0, tiled...  273 us
    another operation x4, other arithmetic, thin_step(): jnp.stack([inner_depth * first_new, inner_depth * second_new], axis=1)  40 us
    ppermute x8, starting transfers between devices, padded(): lax.ppermute(tail, axis, [(i, (i + 1) % count) for i in range(ends)])  32 us
    unnamed x30, local copies, waits for them, and re-layouts  27.9 us
    sub x2, other arithmetic, thin_step(): height_new = height - DIVERGE * divergence  24.1 us
    dot_general x1, matrix products, shards(): updated = center + jnp.dot(weights.T, member_deviations, precision=precise)  17.4 us
    all_to_all x1, local copies, waits for them, and re-layouts, shards(): lax.all_to_all(dynamic_vector, 'grid', split_axis=2, concat_axis=0, tiled...  16.6 us
    another operation x1, local copies, waits for them, and re-layouts, thin_step(): return jnp.stack([height_new, first_new, second_new], axis=1)  12.1 us
  transfers between devices with their start and end apart: 17, of which 7 were waited for; matrix products, arithmetic and copies ran while one was open for 2% of the time, Pallas kernels for 0%

commit v1 on v0

--- a/solution.py
+++ b/solution.py
@@ -11,6 +11,13 @@
 DIVERGE = 0.35
 CORIOLIS = 0.2
 precise = lax.Precision.HIGHEST
+
+
+def trade_parts(x, axis, split, join):
+    size = lax.axis_size(axis)
+    blocks = jnp.stack(jnp.split(x, size, axis=split), axis=0)
+    blocks = lax.all_to_all(blocks, axis, split_axis=0, concat_axis=0)
+    return jnp.concatenate(blocks, axis=join)
 
 
 def padded(cells, sides, width):
@@ -107,7 +114,7 @@
     inner_cor = latitude_coupling[2:-2]
     for number in range(STEPS):
         dynamic_vector = thin_step(dynamic_vector, constant_fields, inner_cor)
-    blocks = lax.all_to_all(dynamic_vector, "grid", split_axis=2, concat_axis=0, tiled=True)
+    blocks = trade_parts(dynamic_vector, "grid", 2, 0)
     packed = domain_reduction(observe(blocks[:, 0], obs_cell, obs_count, obs_value, obs_error))
     weights = transform(packed)
     members = blocks.shape[0]

time: 588 us -> 564 us (0.959)
  local copies, waits for them, and re-layouts: 112 us -> 87.9 us
    all_to_all x1 -> x0, local copies, waits for them, and re-layouts: 16.6 us -> none  [shards(): lax.all_to_all(dynamic_vector, 'grid', split_axis=2, concat_axis=0, tiled...]
    reshape x1 -> x0, local copies, waits for them, and re-layouts: 12 us -> none  [shards(): flat = blocks.reshape(members, -1)]
    another operation x4, other arithmetic: 40 us -> 29.5 us  [thin_step(): jnp.stack([inner_depth * first_new, inner_depth * second_new], axis=1)]
    slice x1 -> x0, local copies, waits for them, and re-layouts: 10.2 us -> none  [thin_step(): dynamic_vector[:, 2]]
    another operation x1 -> x2, local copies, waits for them, and re-layouts: 12.1 us -> 21.5 us  [the longest x1 12 us: shards(): flat = blocks.reshape(members, -1)]
    unnamed x30 -> x24, local copies, waits for them, and re-layouts: 27.9 us -> 18.5 us
    another operation x0 -> x1, other arithmetic: none -> 7.9 us  [trade_parts(): blocks = jnp.stack(jnp.split(x, size, axis=split), axis=0)]
    slice x1 -> x2, local copies, waits for them, and re-layouts: 5 us -> 11.9 us  [shards(): blocks[:, 0]]
  transfers between devices with their start and end apart: 17 -> 17, of which waited for: 7 -> 9; matrix products, arithmetic and copies ran while one was open for 2% -> 2% of each run, Pallas kernels for 0% -> 0%
where the time goes in v1:
time: 564 us; the launch traced here: 554 us
  waiting for transfers between devices  281 us (50%)
  other arithmetic  103 us (18%)
  local copies, waits for them, and re-layouts  87.9 us (16%)
  starting transfers between devices  47.4 us (8%)
  matrix products  21.8 us (4%)
  blocking collectives  11.4 us (2%)
    all_to_all x1, waiting for transfers between devices, trade_parts(): blocks = lax.all_to_all(blocks, axis, split_axis=0, concat_axis=0)  273 us
    ppermute x8, starting transfers between devices, padded(): lax.ppermute(tail, axis, [(i, (i + 1) % count) for i in range(ends)])  30.6 us
    another operation x4, other arithmetic, thin_step(): jnp.stack([inner_depth * first_new, inner_depth * second_new], axis=1)  29.5 us
    sub x2, other arithmetic, thin_step(): height_new = height - DIVERGE * divergence  25.9 us
    unnamed x24, local copies, waits for them, and re-layouts  18.5 us
    dot_general x1, matrix products, shards(): updated = center + jnp.dot(weights.T, member_deviations, precision=precise)  17 us
    another operation x1, local copies, waits for them, and re-layouts, shards(): flat = blocks.reshape(members, -1)  12 us
    slice x2, local copies, waits for them, and re-layouts, shards(): blocks[:, 0]  11.9 us
  transfers between devices with their start and end apart: 17, of which 9 were waited for; matrix products, arithmetic and copies ran while one was open for 2% of the time, Pallas kernels for 0%

profile of v1, /device:TPU:0, one launch (start us, length us, event | category | flops | bytes accessed | tf_op | source)
XLA Modules:
  0.0 554.4 jit_solution(11699586528180589546)
XLA Ops:
  6.3 4.8 collective-permute-start.1
  22.5 14.6 %multiply_bitcast_fusion.3 = (f32[16,1,128,512]{3,2,0,1:T(8,128)S(1)}, f32[16,128,512]{2,1,0:T(8,128)}, f32[16,1,128,512]{3,2,0,1:T(8,128)S(1)}, f32[16,128,512]{2,1,0:T(8,128)}) fusion(f32[128,512]{1,0:T(8,128)} %param.8, f32[16,128,512]{2,1,0:T(8,128)} %copy-done.5, f32[16,1,512]{2,1,0:T(1,128)S(1)} %collective-permute-done.1, ...), kind=kLoop, calls=%fused_computation.83 | loop fusion | flops 25165824 | bytes 29967104 | tf_op jit(solution)/shard_map/stack | solution.py:57
  38.6 4.5 collective-permute-start.5
  62.3 12.8 %bitcast_subtract_fusion.1 = (f32[16,128,512]{2,1,0:T(8,128)S(1)}, f32[16,1,128,512]{3,2,0,1:T(8,128)}) fusion(f32[16,3,128,512]{3,2,1,0:T(8,128)} %param.7, f32[16,2,1,512]{3,2,0,1:T(1,128)S(1)} %collective-permute-done.4, f32[16,1,128,512]{3,2,0,1:T(8,128)} %copy-done.3, f32[16,1,128,512]{3,2,0,1:T(8,128)} %copy-done.2, ...), kind=kLoop, calls=%fused_computation.79 | loop fusion | flops 17825792 | bytes 21135872 | tf_op jit(solution)/shard_map/sub | solution.py:64
  76.5 4.5 collective-permute-start.9
  94.8 14.7 %multiply_bitcast_fusion.1 = (f32[16,1,128,512]{3,2,0,1:T(8,128)S(1)}, f32[16,128,512]{2,1,0:T(8,128)}, f32[16,1,128,512]{3,2,0,1:T(8,128)S(1)}, f32[16,128,512]{2,1,0:T(8,128)}) fusion(f32[128,512]{1,0:T(8,128)} %param.8, f32[16,128,512]{2,1,0:T(8,128)} %copy-done.4, f32[16,1,512]{2,1,0:T(1,128)S(1)} %collective-permute-done.9, ...), kind=kLoop, calls=%fused_computation.81 | loop fusion | flops 25165824 | bytes 29967104 | tf_op jit(solution)/shard_map/stack | solution.py:57
  110.9 4.5 collective-permute-start.13
  117.3 3.1 pad_maximum_fusion.45
  134.7 13.0 %fusion.6 = f32[16,1,128,512]{3,2,1,0:T(8,128)} fusion(f32[16,2,130,1]{3,2,0,1:T(8,128)} %copy.62, f32[16,2,1,512]{3,2,0,1:T(1,128)S(1)} %collective-permute-done.12, f32[16,2,1,512]{3,2,0,1:T(1,128)S(1)} %collective-permute-done.13, f32[16,1,128,512]{3,2,0,1:T(8,128)} %copy-done.1, f32[16,1,128,512]{3,2,0,1:T(8,128)} %copy-done, ...), kind=kLoop, calls=%fused_computation.11 | loop fusion | flops 18874368 | bytes 21135872 | tf_op jit(solution)/shard_map/sub | solution.py:64
  147.7 10.6 %pad_maximum_fusion = f32[16,3,128,512]{3,2,1,0:T(8,128)} fusion(f32[16,1,128,512]{3,2,1,0:T(8,128)} %bitcast.160, f32[16,1,128,512]{3,2,1,0:T(8,128)S(1)} %bitcast.159, f32[16,1,128,512]{3,2,1,0:T(8,128)} %fusion.6), kind=kLoop, calls=%fused_computation.2 | loop fusion | flops 6291456 | bytes 25165824 | tf_op jit(solution)/shard_map/stack | solution.py:65
  158.3 9.5 %slice_bitcast_fusion.4 = (f32[1,16,3,32,512]{4,3,2,1,0:T(8,128)S(1)}, f32[1,16,3,32,512]{4,3,2,1,0:T(8,128)S(1)}, f32[1,16,3,32,512]{4,3,2,1,0:T(8,128)}, f32[1,16,3,32,512]{4,3,2,1,0:T(8,128)}) fusion(f32[16,3,128,512]{3,2,1,0:T(8,128)} %pad_maximum_fusion), kind=kLoop, calls=%fused_computation.88 | loop fusion | bytes 25165824 | tf_op jit(solution)/shard_map/stack | solution.py:18
  167.8 7.9 %pad_maximum_fusion.1 = f32[4,16,3,32,512]{4,3,2,1,0:T(8,128)} fusion(f32[1,16,3,32,512]{4,3,2,1,0:T(8,128)S(1)} %get-tuple-element.20, f32[1,16,3,32,512]{4,3,2,1,0:T(8,128)} %get-tuple-element.21, f32[1,16,3,32,512]{4,3,2,1,0:T(8,128)} %get-tuple-element.22, f32[1,16,3,32,512]{4,3,2,1,0:T(8,128)S(1)} %get-tuple-element.19), kind=kLoop, calls=%fused_computation.3 | loop fusion | flops 9437184 | bytes 25165824 | tf_op jit(solution)/shard_map/stack | solution.py:18
  175.7 6.4 %all-to-all-start = ((f32[4,16,3,32,512]{4,3,2,1,0:T(8,128)}), f32[4,16,3,32,512]{4,3,2,1,0:T(8,128)}, u32[]{:S(2)}, u32[]{:S(2)}) async-start(f32[4,16,3,32,512]{4,3,2,1,0:T(8,128)} %pad_maximum_fusion.1), calls=%async_computation | async-start | bytes 25165824 | tf_op jit(solution)/shard_map/all_to_all | solution.py:19
  183.0 273.2 %all-to-all-done = f32[4,16,3,32,512]{4,3,2,1,0:T(8,128)} async-done(((f32[4,16,3,32,512]{4,3,2,1,0:T(8,128)}), f32[4,16,3,32,512]{4,3,2,1,0:T(8,128)}, u32[]{:S(2)}, u32[]{:S(2)}) %all-to-all-start) | async-done | bytes 12582944 | tf_op jit(solution)/shard_map/all_to_all | solution.py:19
  456.1 4.9 slice.199
  461.1 6.9 %copy.65 = f32[64,1,32,512]{0,3,2,1:T(8,128)} copy(f32[64,1,32,512]{3,2,1,0:T(8,128)} %slice.199) | data formatting | bytes 8388608 | tf_op jit(solution)/shard_map/slice | solution.py:118
  468.0 4.0 gather_fusion
  473.0 11.4 %psum.7 = f32[65,64]{0,1:T(8,128)S(1)} all-reduce(f32[65,64]{0,1:T(8,128)S(1)} %pad_maximum_fusion.60), channel_id=1, replica_groups=mesh['copy'=2,'grid'=4,'blk'=2,'sub'=2] {'blk','sub'}, use_global_device_ids=true, to_apply=%region_2.3 | all-reduce | flops 4160 | bytes 33280 | tf_op jit(solution)/shard_map/psum | solution.py:84
  489.7 5.8 %cholesky.26 = f32[64,64]{1,0:T(8,128)S(1)} custom-call(f32[64,64]{1,0:T(8,128)S(1)} %fusion.42), custom_call_target="Cholesky" | custom-call | tf_op jit(solution)/shard_map/jit(cholesky)/cholesky | solution.py:93
  497.1 4.9 custom-call.10
  502.3 5.8 %reduce_sum.27 = f32[3,32,512]{2,1,0:T(8,128)S(1)} reduce(f32[4,16,3,32,512]{4,3,2,1,0:T(8,128)} %all-to-all-done, f32[]{:T(128)} %constant.91.clone.1), dimensions={0,1}, to_apply=%region_0.1 | reduce | flops 3096576 | bytes 12779524 | tf_op jit(solution)/shard_map/reduce_sum | solution.py:122
  508.5 12.0 %reshape_reshape.3 = f32[64,49152]{1,0:T(8,128)} reshape(f32[4,16,3,32,512]{4,3,2,1,0:T(8,128)} %all-to-all-done) | data formatting | bytes 25165824 | tf_op jit(solution)/shard_map/reshape;reshape | solution.py:121
  520.5 17.0 %convolution_add_fusion = f32[64,49152]{1,0:T(8,128)} fusion(f32[64,64]{1,0:T(8,128)S(1)} %fusion.31, f32[64,49152]{1,0:T(8,128)} %reshape_reshape.3, f32[49152]{0:T(1024)S(1)} %bitcast.162), kind=kOutput, calls=%fused_computation.1 | convolution fusion | flops 2422210560 | bytes 25378816 | tf_op jit(solution)/shard_map/dot_general | solution.py:124
  537.6 16.4 %copy.80 = f32[8,8,96,512]{3,2,1,0:T(8,128)} copy(f32[8,8,96,512]{3,1,2,0:T(8,128)} %bitcast.158) | data formatting | bytes 25165824
  (122 shorter events, 78.4 us)
Async XLA Ops:
  5.0 6.2 %collective-permute-start = (f32[16,1,512]{2,1,0:T(1,128)S(1)}, f32[16,1,512]{2,1,0:T(1,128)S(1)}, u32[]{:S(2)}, u32[]{:S(2)}) collective-permute-start(f32[16,1,512]{2,1,0:T(1,128)S(1)} %get-tuple-element.38), channel_id=1, source_target_pairs={{2,0},{3,1},{6,4},{7,5},{10,8},{11,9},{14,12},{15,13},{18,16},{19,... | collective-permute-start | bytes 98312 | tf_op jit(solution)/shard_map/ppermute | solution.py:33
  6.3 6.4 %collective-permute-start.1 = (f32[16,1,512]{2,1,0:T(1,128)S(1)}, f32[16,1,512]{2,1,0:T(1,128)S(1)}, u32[]{:S(2)}, u32[]{:S(2)}) collective-permute-start(f32[16,1,512]{2,1,0:T(1,128)S(1)} %get-tuple-element.37), channel_id=1, source_target_pairs={{0,2},{1,3},{4,6},{5,7},{8,10},{9,11},{12,14},{13,15},{16,18},{17,... | collective-permute-start | bytes 98312 | tf_op jit(solution)/shard_map/ppermute | solution.py:31
  11.1 9.1 %copy-start.7 = (s32[128,512]{1,0:T(8,128)S(1)}, s32[128,512]{1,0:T(8,128)}, u32[]{:S(2)}) copy-start(s32[128,512]{1,0:T(8,128)} %param.9) | copy-start | bytes 786436
  15.3 5.1 collective-permute-start.2
  17.2 3.9 collective-permute-start.3
  37.2 7.9 %copy-start.2 = (f32[16,1,128,512]{3,2,0,1:T(8,128)}, f32[16,1,128,512]{3,2,0,1:T(8,128)S(1)}, u32[]{:S(2)}) copy-start(f32[16,1,128,512]{3,2,0,1:T(8,128)S(1)} %get-tuple-element.11) | copy-start | bytes 12582916
  37.3 6.2 %collective-permute-start.4 = (f32[16,2,1,512]{3,2,0,1:T(1,128)S(1)}, f32[16,2,1,512]{3,2,0,1:T(1,128)S(1)}, u32[]{:S(2)}, u32[]{:S(2)}) collective-permute-start(f32[16,2,1,512]{3,2,0,1:T(1,128)S(1)} %get-tuple-element.30), channel_id=1, source_target_pairs={{2,0},{3,1},{6,4},{7,5},{10,8},{11,9},{14,12},{15,13},{18,16},{19,... | collective-permute-start | bytes 196616 | tf_op jit(solution)/shard_map/ppermute | solution.py:33
  38.6 6.4 %collective-permute-start.5 = (f32[16,2,1,512]{3,2,0,1:T(1,128)S(1)}, f32[16,2,1,512]{3,2,0,1:T(1,128)S(1)}, u32[]{:S(2)}, u32[]{:S(2)}) collective-permute-start(f32[16,2,1,512]{3,2,0,1:T(1,128)S(1)} %get-tuple-element.29), channel_id=1, source_target_pairs={{0,2},{1,3},{4,6},{5,7},{8,10},{9,11},{12,14},{13,15},{16,18},{17,... | collective-permute-start | bytes 196616 | tf_op jit(solution)/shard_map/ppermute | solution.py:31
  50.9 7.2 %collective-permute-start.6 = (f32[16,2,130,1]{2,0,3,1:T(8,128)S(1)}, f32[16,2,130,1]{2,0,3,1:T(8,128)S(1)}, u32[]{:S(2)}, u32[]{:S(2)}) collective-permute-start(f32[16,2,130,1]{2,0,3,1:T(8,128)S(1)} %copy.51), channel_id=1, source_target_pairs={{1,0},{3,2},{5,4},{7,6},{9,8},{11,10},{13,12},{15,14},{17,16},{19,... | collective-permute-start | bytes 49928 | tf_op jit(solution)/shard_map/ppermute | solution.py:33
  55.0 5.2 collective-permute-start.7
  75.2 5.9 %collective-permute-start.8 = (f32[16,1,512]{2,1,0:T(1,128)S(1)}, f32[16,1,512]{2,1,0:T(1,128)S(1)}, u32[]{:S(2)}, u32[]{:S(2)}) collective-permute-start(f32[16,1,512]{2,1,0:T(1,128)S(1)} %get-tuple-element.36), channel_id=1, source_target_pairs={{2,0},{3,1},{6,4},{7,5},{10,8},{11,9},{14,12},{15,13},{18,16},{19,... | collective-permute-start | bytes 98312 | tf_op jit(solution)/shard_map/ppermute | solution.py:33
  76.5 6.1 %collective-permute-start.9 = (f32[16,1,512]{2,1,0:T(1,128)S(1)}, f32[16,1,512]{2,1,0:T(1,128)S(1)}, u32[]{:S(2)}, u32[]{:S(2)}) collective-permute-start(f32[16,1,512]{2,1,0:T(1,128)S(1)} %get-tuple-element.35), channel_id=1, source_target_pairs={{0,2},{1,3},{4,6},{5,7},{8,10},{9,11},{12,14},{13,15},{16,18},{17,... | collective-permute-start | bytes 98312 | tf_op jit(solution)/shard_map/ppermute | solution.py:31
  86.3 6.2 %collective-permute-start.10 = (f32[16,130,1]{1,0,2:T(8,128)S(1)}, f32[16,130,1]{1,0,2:T(8,128)S(1)}, u32[]{:S(2)}, u32[]{:S(2)}) collective-permute-start(f32[16,130,1]{1,0,2:T(8,128)S(1)} %copy.55), channel_id=1, source_target_pairs={{1,0},{3,2},{5,4},{7,6},{9,8},{11,10},{13,12},{15,14},{17,16},{19,... | collective-permute-start | bytes 24968 | tf_op jit(solution)/shard_map/ppermute | solution.py:33
  89.5 3.9 collective-permute-start.11
  109.4 7.9 %copy-start = (f32[16,1,128,512]{3,2,0,1:T(8,128)}, f32[16,1,128,512]{3,2,0,1:T(8,128)S(1)}, u32[]{:S(2)}) copy-start(f32[16,1,128,512]{3,2,0,1:T(8,128)S(1)} %get-tuple-element.5) | copy-start | bytes 12582916
  109.5 7.9 %copy-start.1 = (f32[16,1,128,512]{3,2,0,1:T(8,128)}, f32[16,1,128,512]{3,2,0,1:T(8,128)S(1)}, u32[]{:S(2)}) copy-start(f32[16,1,128,512]{3,2,0,1:T(8,128)S(1)} %get-tuple-element.17) | copy-start | bytes 12582916
  109.6 6.2 %collective-permute-start.12 = (f32[16,2,1,512]{3,2,0,1:T(1,128)S(1)}, f32[16,2,1,512]{3,2,0,1:T(1,128)S(1)}, u32[]{:S(2)}, u32[]{:S(2)}) collective-permute-start(f32[16,2,1,512]{3,2,0,1:T(1,128)S(1)} %get-tuple-element.28), channel_id=1, source_target_pairs={{2,0},{3,1},{6,4},{7,5},{10,8},{11,9},{14,12},{15,13},{18,16},{19,... | collective-permute-start | bytes 196616 | tf_op jit(solution)/shard_map/ppermute | solution.py:33
  110.9 6.4 %collective-permute-start.13 = (f32[16,2,1,512]{3,2,0,1:T(1,128)S(1)}, f32[16,2,1,512]{3,2,0,1:T(1,128)S(1)}, u32[]{:S(2)}, u32[]{:S(2)}) collective-permute-start(f32[16,2,1,512]{3,2,0,1:T(1,128)S(1)} %get-tuple-element.27), channel_id=1, source_target_pairs={{0,2},{1,3},{4,6},{5,7},{8,10},{9,11},{12,14},{13,15},{16,18},{17,... | collective-permute-start | bytes 196616 | tf_op jit(solution)/shard_map/ppermute | solution.py:31
  123.2 7.2 %collective-permute-start.14 = (f32[16,2,130,1]{2,0,3,1:T(8,128)S(1)}, f32[16,2,130,1]{2,0,3,1:T(8,128)S(1)}, u32[]{:S(2)}, u32[]{:S(2)}) collective-permute-start(f32[16,2,130,1]{2,0,3,1:T(8,128)S(1)} %copy.59), channel_id=1, source_target_pairs={{1,0},{3,2},{5,4},{7,6},{9,8},{11,10},{13,12},{15,14},{17,16},{19,... | collective-permute-start | bytes 49928 | tf_op jit(solution)/shard_map/ppermute | solution.py:33
  127.3 5.2 collective-permute-start.15
  134.7 13.0 %copy-start.6 = (f32[16,128,512]{2,1,0:T(8,128)S(1)}, f32[16,128,512]{2,1,0:T(8,128)}, u32[]{:S(2)}) copy-start(f32[16,128,512]{2,1,0:T(8,128)} %get-tuple-element.6) | copy-start | bytes 12582916
  175.7 280.4 %all-to-all-start = ((f32[4,16,3,32,512]{4,3,2,1,0:T(8,128)}), f32[4,16,3,32,512]{4,3,2,1,0:T(8,128)}, u32[]{:S(2)}, u32[]{:S(2)}) async-start(f32[4,16,3,32,512]{4,3,2,1,0:T(8,128)} %pad_maximum_fusion.1), calls=%async_computation | async-start | bytes 25165824 | tf_op jit(solution)/shard_map/all_to_all | solution.py:19
  461.1 11.1 %copy-start.8 = (f32[1,1,1,64]{3,2,1,0:T(1,128)S(1)}, f32[1,1,1,64]{3,2,1,0:T(1,128)}, u32[]{:S(2)}) copy-start(f32[1,1,1,64]{3,2,1,0:T(1,128)} %param.13) | copy-start | bytes 772
  461.1 11.5 %copy-start.10 = (f32[1,1,1,64]{3,2,1,0:T(1,128)S(1)}, f32[1,1,1,64]{3,2,1,0:T(1,128)}, u32[]{:S(2)}) copy-start(f32[1,1,1,64]{3,2,1,0:T(1,128)} %param.12) | copy-start | bytes 772
  (4 other events, 24.6 us)
